TPU v7x, 512 devices: a whole 4x4x16 slice. The times are simulated.
512 devices in a mesh: dom: 8 (over z_lo), orb: 64 (over x, y, z_hi, core).
Axes of the slice: x: 4, y: 4, z: 16 (z_hi: 2, z_lo: 8; z = z_hi * 8 + z_lo), core: 2. Of those that a mesh axis runs over, the one named last changes fastest.
Arguments:
- orbitals: float32 [8, 320, 12, 16, 128], P('dom', 'orb'), may hold values from -6 to 6
- potential: float32 [8, 12, 16, 128], P('dom'), may hold values from -3 to 0
- projectors: float32 [16, 8, 512], replicated, may hold values from -0.25 to 0.25
- projector_energy: float32 [8], replicated, may hold values from 20 to 160
- atom_first: int32 [16], replicated, may hold values from 0 to 23
- atom_second: int32 [16], replicated, may hold values from 0 to 31
- atom_third: int32 [16], replicated, may hold values from 0 to 255
- rotation: bfloat16 [320, 320], P('orb'), may hold values from -0.3125 to 0.3125
Outputs:
- rotated: bfloat16 [8, 320, 12, 16, 128], P('dom', 'orb')
All inputs are finite; a program needn't handle non-finite values.
Results may differ from a plain program's by a relative error of at most 0.0049.
Values may be sent and summed in bfloat16 or wider, within the bound.
A program may use at most 64 MiB of HBM per device.

v0:
```python
import jax
import jax.numpy as jnp
import numpy as np
from jax import lax
from jax.sharding import PartitionSpec as P

SIDE = 8
SUP = 512
stencil_weights = (
    -5369.0 / 1800.0,
    12.0 / 7.0,
    -15.0 / 56.0,
    10.0 / 189.0,
    -1.0 / 112.0,
    2.0 / 1925.0,
    -1.0 / 16632.0,
)
inverse_spacing = 4.0
filter_center = 120.0
filter_width = 110.0
stencil_reach = 6


def partner_2(block, axis, bit):
    count = lax.axis_size(axis)
    route = []
    for low in range(count):
        high = low | 1 << bit
        if high != low and high < count:
            route += [(low, high), (high, low)]
    return lax.ppermute(block, axis, route)


def outgoing(values, direction, width):
    extent = values.shape[direction]
    if 2 * width < extent:
        return jnp.concatenate(
            (
                lax.slice_in_dim(values, 0, width, axis=direction),
                lax.slice_in_dim(values, extent - width, extent, axis=direction),
            ),
            axis=direction,
        )
    return values


def assemble(values, partner, direction, width):
    extent = values.shape[direction]
    if 2 * width < extent:
        lower_rim = lax.slice_in_dim(partner, width, 2 * width, axis=direction)
        upper_rim = lax.slice_in_dim(partner, 0, width, axis=direction)
        return jnp.concatenate((lower_rim, values, upper_rim), axis=direction)
    cyclic = jnp.concatenate((values, partner), axis=direction)
    chosen = np.arange(-width, extent + width) % (2 * extent)
    return jnp.take(cyclic, jnp.asarray(chosen, dtype=jnp.int32), axis=direction)


def face_padded(values, direction, bit_number):
    sent = outgoing(values, direction, stencil_reach)
    partner = partner_2(sent.astype(jnp.bfloat16), "dom", bit_number).astype(sent.dtype)
    return assemble(values, partner, direction, stencil_reach)


def stencil_sum(center, along):
    lead = center.ndim - 3
    summed = 3.0 * stencil_weights[0] * center
    for index in range(3):
        direction = lead + index
        extent = center.shape[direction]
        padded = along[index]
        for offset in range(1, 7):
            upward = lax.slice_in_dim(
                padded, stencil_reach + offset, stencil_reach + offset + extent, axis=direction
            )
            downward = lax.slice_in_dim(
                padded, stencil_reach - offset, stencil_reach - offset + extent, axis=direction
            )
            summed = summed + stencil_weights[offset] * (upward + downward)
    return summed


def support_map(atom_coords, starts, extents, periods):
    offsets = jnp.arange(SIDE, dtype=jnp.int32) - SIDE // 2
    clipped_list = []
    inside_list = []
    for index in range(3):
        local = (atom_coords[index][:, None] + offsets[None, :] - starts[index]) % periods[index]
        inside_list.append(local < extents[index])
        clipped_list.append(jnp.minimum(local, extents[index] - 1))
    inside = (
        inside_list[0][:, :, None, None]
        & inside_list[1][:, None, :, None]
        & inside_list[2][:, None, None, :]
    )
    flattened = (
        clipped_list[0][:, :, None, None] * extents[1] + clipped_list[1][:, None, :, None]
    ) * extents[2] + clipped_list[2][:, None, None, :]
    atom_count = atom_coords[0].shape[0]
    return (
        flattened.reshape(atom_count * SUP),
        inside.reshape(atom_count, SUP).astype(jnp.float32),
    )


def coefficients(values, support, inside, projectors):
    orbital_count = values.shape[0]
    atom_count = projectors.shape[0]
    flattened = values.reshape(orbital_count, -1)
    picked = (
        jnp.take(flattened, support, axis=1).reshape(orbital_count, atom_count, SUP) * inside[None]
    )
    partial_coeffs = jnp.einsum("aps,kas->kap", projectors, picked, precision=lax.Precision.HIGHEST)
    return lax.psum(partial_coeffs, "dom")


def spread_into(coeffs, shape, support, inside, projectors, projector_energy):
    orbital_count = shape[0]
    atom_count = projectors.shape[0]
    scaled = coeffs * projector_energy[None, None, :]
    spread = (
        jnp.einsum("aps,kap->kas", projectors, scaled, precision=lax.Precision.HIGHEST)
        * inside[None]
    )
    total_cells = shape[1] * shape[2] * shape[3]
    projected_part = (
        jnp.zeros((orbital_count, total_cells), jnp.float32)
        .at[:, support]
        .add(spread.reshape(orbital_count, atom_count * SUP))
    )
    return projected_part.reshape(shape)


def own_hamiltonian(center, along, local_field, support, inside, projectors, projector_energy):
    kinetic = -0.5 * inverse_spacing * inverse_spacing
    coeffs = coefficients(center, support, inside, projectors)
    projected_part = spread_into(
        coeffs, center.shape, support, inside, projectors, projector_energy
    )
    return kinetic * stencil_sum(center, along) + local_field[None] * center + projected_part


def body(
    orbitals, potential, projectors, projector_energy, atom_first, atom_second, atom_third, rotation
):
    domain_count = lax.axis_size("dom")
    domain_bits = domain_count.bit_length() - 1
    split = [index < domain_bits for index in range(3)]
    start_values = orbitals[0]
    local_field = potential[0]
    extents = start_values.shape[1:]
    periods = (
        extents[0] * min(domain_count, 2),
        extents[1] * min(max(domain_count // 2, 1), 2),
        extents[2] * max(domain_count // 4, 1),
    )
    domain_index = lax.axis_index("dom")
    anchors = (
        domain_index % 2 * extents[0],
        domain_index // 2 % 2 * extents[1],
        domain_index // 4 * extents[2],
    )
    atom_coords = (atom_first, atom_second, atom_third)
    support, inside = support_map(atom_coords, anchors, extents, periods)
    along = [face_padded(start_values, index + 1, index) for index in range(3)]
    first_apply = own_hamiltonian(
        start_values, along, local_field, support, inside, projectors, projector_energy
    )
    first_term = (first_apply - filter_center * start_values) / filter_width
    along = [face_padded(first_term, index + 1, index) for index in range(3)]
    second_apply = own_hamiltonian(
        first_term, along, local_field, support, inside, projectors, projector_energy
    )
    second_term = 2.0 * (second_apply - filter_center * first_term) / filter_width - start_values
    per_device = start_values.shape[0]
    filtered = second_term.astype(jnp.bfloat16).reshape(per_device, -1)
    by_cells = lax.all_to_all(filtered, "orb", split_axis=1, concat_axis=0, tiled=True)
    whole_rotation = lax.all_gather(rotation, "orb", axis=0, tiled=True)
    rotated = lax.dot_general(
        whole_rotation, by_cells, (((0,), (0,)), ((), ())), preferred_element_type=jnp.float32
    ).astype(jnp.bfloat16)
    result = lax.all_to_all(rotated, "orb", split_axis=0, concat_axis=1, tiled=True)
    return result.reshape((1,) + start_values.shape)


def solution(mesh):
    return jax.shard_map(
        body,
        mesh=mesh,
        in_specs=(
            P("dom", "orb", None, None, None),
            P("dom", None, None, None),
            P(),
            P(),
            P(),
            P(),
            P(),
            P("orb", None),
        ),
        out_specs=P("dom", "orb", None, None, None),
        check_vma=False,
    )
```

profile of v0, /device:TPU:1, one launch (start us, length us, event | category | flops | bytes accessed | tf_op | source)
XLA Modules:
  0.0 617.4 jit_solution(15906306912854920774)
XLA Ops:
  0.0 1.1 copy.95
  1.1 4.4 collective-permute-start
  5.8 8.8 %collective-permute-start.2 = (bf16[5,12,16,12]{3,2,0,1:T(8,128)(2,1)S(1)}, bf16[5,12,16,12]{3,2,0,1:T(8,128)(2,1)S(1)}, u32[]{:S(2)}, u32[]{:S(2)}) collective-permute-start(bf16[5,12,16,12]{3,2,0,1:T(8,128)(2,1)S(1)} %pad_maximum_fusion.11), channel_id=1, source_target_pairs={{0,256},{256,0},{64,320},{320,64},{128,384},{384,128},{192,448},{4... | collective-permute-start | bytes 69128 | tf_op jit(solution)/shard_map/ppermute | solution.py:31
  15.5 4.9 collective-permute-start.1
  22.0 7.9 %copy.69 = f32[1,5,12,16,128]{1,4,3,2,0:T(8,128)} copy(f32[1,5,12,16,128]{4,3,2,1,0:T(8,128)} %param.14) | data formatting | bytes 983040 | tf_op args[0]
  31.2 32.3 %gather_fusion.1 = f32[8192,5]{1,0:T(8,128)} fusion(f32[5,24576]{0,1:T(8,128)} %bitcast.59, s32[8192]{0:T(1024)S(1)} %fusion.157), kind=kCustom, calls=%fused_computation.1.clone | custom fusion | bytes 360448 | tf_op jit(solution)/shard_map/jit(_take)/gather | solution.py:110
  63.5 7.5 %broadcast_select_fusion.1 = f32[8192,5]{1,0:T(8,128)} fusion(f32[8192,5]{1,0:T(8,128)} %gather_fusion.1, pred[8192]{0:T(1024)(128)(4,1)S(1)} %compare_and_fusion), kind=kLoop, calls=%fused_computation.11 | loop fusion | flops 40960 | bytes 335872 | tf_op jit(solution)/shard_map/jit(_take)/select_n | solution.py:110
  70.9 2.9 copy.71
  74.5 42.7 %psum.14 = f32[5,16,8]{2,0,1:T(8,128)S(1)} all-reduce(f32[5,16,8]{2,0,1:T(8,128)S(1)} %convolution_bitcast_fusion.1), channel_id=1, replica_groups=mesh['dom'=8,'orb'=64] {'dom'}, use_global_device_ids=true, to_apply=%region_0.3 | all-reduce | flops 640 | bytes 5120 | tf_op jit(solution)/shard_map/psum | solution.py:113
  118.3 2.6 copy.73
  120.9 54.2 %scatter_custom_fusion = f32[5,24576]{0,1:T(8,128)} fusion(s32[8192]{0:T(1024)S(1)} %bitcast.74, f32[8192,5]{1,0:T(8,128)} %copy.73, f32[]{:T(128)} %constant.127.clone.1), kind=kCustom, calls=%fused_computation.8 | custom fusion | flops 40960 | bytes 492032 | tf_op jit(solution)/shard_map/scatter-add | solution.py:128
  175.1 8.3 %copy.74 = f32[5,12,16,128]{3,2,0,1:T(8,128)} copy(f32[5,12,16,128]{0,3,2,1:T(8,128)} %bitcast.56) | data formatting | bytes 983040 | tf_op jit(solution)/shard_map/reshape | solution.py:130
  186.0 6.8 %fusion.168 = (bf16[5,12,16,128]{3,2,0,1:T(8,128)(2,1)S(1)}, f32[5,12,16,128]{3,2,0,1:T(8,128)S(1)}) fusion(f32[5,12,16,128]{3,2,0,1:T(8,128)S(1)} %bitcast.64, f32[5,12,16,128]{3,2,0,1:T(8,128)} %copy.74, f32[12,16,128]{2,1,0:T(8,128)} %bitcast.73, f32[5,12,16,6]{3,2,0,1:T(8,128)} %get-tuple-element.22, f32[5,12,16,6]{3,2,0,1:T(8,128)} %get-tuple-element.21, ...), kind=kLoop, calls=%fused_computation.309 | loop fusion | flops 10690560 | bytes 8131584 | tf_op jit(solution)/shard_map/convert_element_type | solution.py:60
  193.0 2.1 collective-permute-start.3
  195.2 6.6 %copy.85 = f32[5,12,16,128]{0,3,2,1:T(8,128)} copy(f32[5,12,16,128]{3,2,0,1:T(8,128)S(1)} %broadcast_multiply_fusion) | data formatting | bytes 983040 | tf_op jit(solution)/shard_map/reshape | solution.py:108
  201.8 32.3 %gather_fusion.3 = f32[8192,5]{1,0:T(8,128)} fusion(f32[5,24576]{0,1:T(8,128)} %bitcast.60, s32[8192]{0:T(1024)S(1)} %fusion.157), kind=kCustom, calls=%fused_computation.3.clone | custom fusion | bytes 360448 | tf_op jit(solution)/shard_map/jit(_take)/gather | solution.py:110
  234.1 7.5 %broadcast_select_fusion = f32[8192,5]{1,0:T(8,128)} fusion(f32[8192,5]{1,0:T(8,128)} %gather_fusion.3, pred[8192]{0:T(1024)(128)(4,1)S(1)} %compare_and_fusion), kind=kLoop, calls=%fused_computation.10 | loop fusion | flops 40960 | bytes 335872 | tf_op jit(solution)/shard_map/jit(_take)/select_n | solution.py:110
  241.5 2.8 copy.78
  245.0 43.8 %psum.15 = f32[5,16,8]{2,0,1:T(8,128)S(1)} all-reduce(f32[5,16,8]{2,0,1:T(8,128)S(1)} %convolution_bitcast_fusion), channel_id=1, replica_groups=mesh['dom'=8,'orb'=64] {'dom'}, use_global_device_ids=true, to_apply=%region_2.5 | all-reduce | flops 640 | bytes 5120 | tf_op jit(solution)/shard_map/psum | solution.py:113
  290.0 1.9 collective-permute-start.5
  292.0 2.6 copy.79
  294.7 54.2 %scatter_custom_fusion.1 = f32[5,24576]{0,1:T(8,128)} fusion(s32[8192]{0:T(1024)} %bitcast.75, f32[8192,5]{1,0:T(8,128)} %copy.79, f32[]{:T(128)} %constant.127.clone.1), kind=kCustom, calls=%fused_computation.6 | custom fusion | flops 40960 | bytes 492032 | tf_op jit(solution)/shard_map/scatter-add | solution.py:128
  348.9 7.6 %copy.81 = f32[5,12,16,128]{3,2,0,1:T(8,128)S(1)} copy(f32[5,12,16,128]{0,3,2,1:T(8,128)} %bitcast.55) | data formatting | bytes 983040 | tf_op jit(solution)/shard_map/reshape | solution.py:130
  356.5 2.4 collective-permute-start.4
  358.9 1.1 fusion.173
  360.0 5.0 collective-permute-done.4
  366.8 1.0 copy.75
  367.9 1.9 gather_fusion.2
  369.8 7.5 %subtract_convert_fusion = bf16[5,12,16,128]{3,2,0,1:T(8,128)(2,1)S(1)} fusion(f32[5,12,16,128]{3,2,0,1:T(8,128)S(1)} %get-tuple-element.8, f32[5,12,16,128]{3,2,0,1:T(8,128)S(1)} %copy.81, f32[5,12,16,128]{3,2,0,1:T(8,128)S(1)} %broadcast_multiply_fusion, f32[5,12,16,6]{3,2,0,1:T(8,128)} %get-tuple-element.14, f32[5,12,16,6]{3,2,0,1:T(8,128)} %get-tuple-element.13, ...), kind=kLoop, calls=%fused_computation.265 | loop fusion | flops 10813440 | bytes 8623104 | tf_op jit(solution)/shard_map/convert_element_type | solution.py:175
  378.4 34.7 %all-to-all-start = ((bf16[5,64,384]{2,0,1:T(8,128)(2,1)}), bf16[5,64,384]{2,0,1:T(8,128)(2,1)S(1)}, u32[]{:S(2)}, u32[]{:S(2)}) async-start(bf16[5,64,384]{2,0,1:T(8,128)(2,1)} %copy.83), calls=%async_computation | async-start | bytes 786432 | tf_op jit(solution)/shard_map/all_to_all | solution.py:176
  413.1 172.7 %all-gather = bf16[64,5,320]{2,1,0:T(8,128)(2,1)S(1)} all-gather(bf16[1,5,320]{2,1,0:T(8,128)(2,1)} %bitcast.76), channel_id=1, replica_groups=mesh['dom'=8,'orb'=64] {'orb'}, dimensions={0}, use_global_device_ids=true | all-gather | bytes 208000 | tf_op jit(solution)/shard_map/all_gather | solution.py:177
  586.5 30.0 %all_to_all.35 = bf16[64,5,384]{2,1,0:T(8,128)(2,1)S(1)} all-to-all(bf16[64,5,384]{2,1,0:T(8,128)(2,1)S(1)} %all_to_all.30), channel_id=1, replica_groups=mesh['dom'=8,'orb'=64] {'orb'}, dimensions={0} | all-to-all | bytes 491520 | tf_op jit(solution)/shard_map/all_to_all | solution.py:181
  (71 shorter events, 14.7 us)
Async XLA Ops:
  0.0 73.8 %copy-start = (f32[16,8,512]{2,1,0:T(8,128)S(1)}, f32[16,8,512]{2,1,0:T(8,128)}, u32[]{:S(2)}) copy-start(f32[16,8,512]{2,1,0:T(8,128)} %param.16) | copy-start | bytes 786436
  1.1 184.1 %collective-permute-start = (bf16[5,12,16,128]{3,2,0,1:T(8,128)(2,1)S(1)}, bf16[5,12,16,128]{3,2,0,1:T(8,128)(2,1)S(1)}, u32[]{:S(2)}, u32[]{:S(2)}) collective-permute-start(bf16[5,12,16,128]{3,2,0,1:T(8,128)(2,1)S(1)} %bitcast.65), channel_id=1, source_target_pairs={{0,64},{64,0},{128,192},{192,128},{256,320},{320,256},{384,448},{4... | collective-permute-start | bytes 737288 | tf_op jit(solution)/shard_map/ppermute | solution.py:31
  5.8 177.7 %collective-permute-start.2 = (bf16[5,12,16,12]{3,2,0,1:T(8,128)(2,1)S(1)}, bf16[5,12,16,12]{3,2,0,1:T(8,128)(2,1)S(1)}, u32[]{:S(2)}, u32[]{:S(2)}) collective-permute-start(bf16[5,12,16,12]{3,2,0,1:T(8,128)(2,1)S(1)} %pad_maximum_fusion.11), channel_id=1, source_target_pairs={{0,256},{256,0},{64,320},{320,64},{128,384},{384,128},{192,448},{4... | collective-permute-start | bytes 69128 | tf_op jit(solution)/shard_map/ppermute | solution.py:31
  15.5 169.0 %collective-permute-start.1 = (bf16[5,12,12,128]{3,2,0,1:T(8,128)(2,1)}, bf16[5,12,12,128]{3,2,0,1:T(8,128)(2,1)S(1)}, u32[]{:S(2)}, u32[]{:S(2)}) collective-permute-start(bf16[5,12,12,128]{3,2,0,1:T(8,128)(2,1)} %pad_maximum_fusion.10), channel_id=1, source_target_pairs={{0,128},{128,0},{64,192},{192,64},{256,384},{384,256},{320,448},{4... | collective-permute-start | bytes 552968 | tf_op jit(solution)/shard_map/ppermute | solution.py:31
  31.0 89.9 %copy-start.4 = (s32[8192,1]{0,1:T(1,128)}, s32[8192,1]{0,1:T(1,128)S(1)}, u32[]{:S(2)}) copy-start(s32[8192,1]{0,1:T(1,128)S(1)} %compare_select_fusion) | copy-start | bytes 98308
  70.9 46.2 %copy-start.2 = (f32[1,12,16,128]{3,2,1,0:T(8,128)S(1)}, f32[1,12,16,128]{3,2,1,0:T(8,128)}, u32[]{:S(2)}) copy-start(f32[1,12,16,128]{3,2,1,0:T(8,128)} %param.15) | copy-start | bytes 294916
  70.9 46.9 %copy-start.6 = (f32[8]{0:T(128)S(1)}, f32[8]{0:T(128)}, u32[]{:S(2)}) copy-start(f32[8]{0:T(128)} %param.17) | copy-start | bytes 100
  70.9 47.3 %copy-start.7 = (s32[24]{0:T(128)S(1)}, s32[24]{0:T(128)}, u32[]{:S(2)}) copy-start(s32[24]{0:T(128)} %constant.175) | copy-start | bytes 292
  70.9 47.3 %copy-start.1 = (f32[1,5,12,16,128]{4,3,2,1,0:T(8,128)S(1)}, f32[1,5,12,16,128]{4,3,2,1,0:T(8,128)}, u32[]{:S(2)}) copy-start(f32[1,5,12,16,128]{4,3,2,1,0:T(8,128)} %param.14) | copy-start | bytes 1474564
  118.2 67.1 %copy-start.5 = (s32[1024]{0:T(1024)}, s32[1024]{0:T(1024)S(1)}, u32[]{:S(2)}) copy-start(s32[1024]{0:T(1024)S(1)} %pad_clamp_fusion) | copy-start | bytes 12292
  193.0 172.8 %collective-permute-start.3 = (bf16[5,12,16,128]{3,2,0,1:T(8,128)(2,1)S(1)}, bf16[5,12,16,128]{3,2,0,1:T(8,128)(2,1)}, u32[]{:S(2)}, u32[]{:S(2)}) collective-permute-start(bf16[5,12,16,128]{3,2,0,1:T(8,128)(2,1)S(1)} %get-tuple-element.6), channel_id=1, source_target_pairs={{0,64},{64,0},{128,192},{192,128},{256,320},{320,256},{384,448},{4... | collective-permute-start | bytes 737288 | tf_op jit(solution)/shard_map/ppermute | solution.py:31
  290.0 68.9 %collective-permute-start.5 = (bf16[5,12,16,12]{3,2,0,1:T(8,128)(2,1)}, bf16[5,12,16,12]{3,2,0,1:T(8,128)(2,1)S(1)}, u32[]{:S(2)}, u32[]{:S(2)}) collective-permute-start(bf16[5,12,16,12]{3,2,0,1:T(8,128)(2,1)} %pad_maximum_fusion.13), channel_id=1, source_target_pairs={{0,256},{256,0},{64,320},{320,64},{128,384},{384,128},{192,448},{4... | collective-permute-start | bytes 69128 | tf_op jit(solution)/shard_map/ppermute | solution.py:31
  356.5 8.5 %collective-permute-start.4 = (bf16[5,12,12,128]{3,2,0,1:T(8,128)(2,1)S(1)}, bf16[5,12,12,128]{3,2,0,1:T(8,128)(2,1)S(1)}, u32[]{:S(2)}, u32[]{:S(2)}) collective-permute-start(bf16[5,12,12,128]{3,2,0,1:T(8,128)(2,1)S(1)} %pad_maximum_fusion.12), channel_id=1, source_target_pairs={{0,128},{128,0},{64,192},{192,64},{256,384},{384,256},{320,448},{4... | collective-permute-start | bytes 552968 | tf_op jit(solution)/shard_map/ppermute | solution.py:31
  360.0 9.8 %copy-start.3 = (f32[12,16,128]{2,1,0:T(8,128)S(1)}, f32[12,16,128]{2,1,0:T(8,128)}, u32[]{:S(2)}) copy-start(f32[12,16,128]{2,1,0:T(8,128)} %broadcast_multiply_fusion.1) | copy-start | bytes 294916
  378.4 207.5 %all-to-all-start = ((bf16[5,64,384]{2,0,1:T(8,128)(2,1)}), bf16[5,64,384]{2,0,1:T(8,128)(2,1)S(1)}, u32[]{:S(2)}, u32[]{:S(2)}) async-start(bf16[5,64,384]{2,0,1:T(8,128)(2,1)} %copy.83), calls=%async_computation | async-start | bytes 786432 | tf_op jit(solution)/shard_map/all_to_all | solution.py:176
where the time goes:
time: 619 us; the launch traced here: 617 us
  blocking collectives  289 us (47%)
  other arithmetic  143 us (23%)
  local copies, waits for them, and re-layouts  118 us (19%)
  starting transfers between devices  59.1 us (10%)
    all_gather x1, blocking collectives, body(): whole_rotation = lax.all_gather(rotation, 'orb', axis=0, tiled=True)  173 us
    scatter-add x2, other arithmetic, spread_into(): projected_part = jnp.zeros((orbital_count, total_cells), jnp.float32).at[...  108 us
    psum x2, blocking collectives, coefficients(): return lax.psum(partial_coeffs, 'dom')  86.5 us
    gather x2, local copies, waits for them, and re-layouts, coefficients(): jnp.take(flattened, support, axis=1).reshape(orbital_count, atom_count, SUP)  64.6 us
    all_to_all x1, starting transfers between devices, body(): lax.all_to_all(filtered, 'orb', split_axis=1, concat_axis=0, tiled=True)  34.7 us
    all_to_all x1, blocking collectives, body(): lax.all_to_all(rotated, 'orb', split_axis=0, concat_axis=1, tiled=True)  30 us
    ppermute x6, starting transfers between devices, partner_2(): return lax.ppermute(block, axis, route)  24.5 us
    reshape x2, local copies, waits for them, and re-layouts, spread_into(): return projected_part.reshape(shape)  15.9 us
  transfers between devices with their start and end apart: 7, of which 1 were waited for; matrix products, arithmetic and copies ran while one was open for 39% of the time, Pallas kernels for 0%

commit v1 on v0

--- a/solution.py
+++ b/solution.py
@@ -110,7 +110,7 @@
         jnp.take(flattened, support, axis=1).reshape(orbital_count, atom_count, SUP) * inside[None]
     )
     partial_coeffs = jnp.einsum("aps,kas->kap", projectors, picked, precision=lax.Precision.HIGHEST)
-    return lax.psum(partial_coeffs, "dom")
+    return jnp.sum(lax.all_gather(partial_coeffs, "dom"), axis=0)
 
 
 def spread_into(coeffs, shape, support, inside, projectors, projector_energy):

time: 619 us -> 607 us (0.981); the launches traced: 617 us -> 598 us
  blocking collectives: 289 us -> 274 us
    psum x2 -> x0, blocking collectives: 86.5 us -> none  [coefficients(): return lax.psum(partial_coeffs, 'dom')]
    all_gather x0 -> x2, blocking collectives: none -> 80.5 us  [coefficients(): return jnp.sum(lax.all_gather(partial_coeffs, 'dom'), axis=0)]
    all_to_all x1, blocking collectives: 30 us -> 23.8 us  [body(): lax.all_to_all(rotated, 'orb', split_axis=0, concat_axis=1, tiled=True)]
  transfers between devices with their start and end apart: 7 -> 7, of which waited for: 1 -> 1; matrix products, arithmetic and copies ran while one was open for 39% -> 40% of each run, Pallas kernels for 0% -> 0%
where the time goes in v1:
time: 607 us; the launch traced here: 598 us
  blocking collectives  274 us (45%)
  other arithmetic  142 us (23%)
  local copies, waits for them, and re-layouts  119 us (20%)
  starting transfers between devices  53.9 us (9%)
    all_gather x1, blocking collectives, body(): whole_rotation = lax.all_gather(rotation, 'orb', axis=0, tiled=True)  170 us
    scatter-add x2, other arithmetic, spread_into(): projected_part = jnp.zeros((orbital_count, total_cells), jnp.float32).at[...  108 us
    all_gather x2, blocking collectives, coefficients(): return jnp.sum(lax.all_gather(partial_coeffs, 'dom'), axis=0)  80.5 us
    gather x2, local copies, waits for them, and re-layouts, coefficients(): jnp.take(flattened, support, axis=1).reshape(orbital_count, atom_count, SUP)  64.9 us
    all_to_all x1, starting transfers between devices, body(): lax.all_to_all(filtered, 'orb', split_axis=1, concat_axis=0, tiled=True)  29.4 us
    ppermute x6, starting transfers between devices, partner_2(): return lax.ppermute(block, axis, route)  24.5 us
    all_to_all x1, blocking collectives, body(): lax.all_to_all(rotated, 'orb', split_axis=0, concat_axis=1, tiled=True)  23.8 us
    reshape x2, local copies, waits for them, and re-layouts, spread_into(): return projected_part.reshape(shape)  15.9 us
  transfers between devices with their start and end apart: 7, of which 1 were waited for; matrix products, arithmetic and copies ran while one was open for 40% of the time, Pallas kernels for 0%

profile of v1, /device:TPU:1, one launch (start us, length us, event | category | flops | bytes accessed | tf_op | source)
XLA Modules:
  0.0 598.0 jit_solution(10635500518361943930)
XLA Ops:
  0.0 1.1 copy.107
  1.1 4.4 collective-permute-start
  5.8 8.8 %collective-permute-start.2 = (bf16[5,12,16,12]{3,2,0,1:T(8,128)(2,1)S(1)}, bf16[5,12,16,12]{3,2,0,1:T(8,128)(2,1)S(1)}, u32[]{:S(2)}, u32[]{:S(2)}) collective-permute-start(bf16[5,12,16,12]{3,2,0,1:T(8,128)(2,1)S(1)} %pad_maximum_fusion.11), channel_id=1, source_target_pairs={{0,256},{256,0},{64,320},{320,64},{128,384},{384,128},{192,448},{4... | collective-permute-start | bytes 69128 | tf_op jit(solution)/shard_map/ppermute | solution.py:31
  15.5 4.9 collective-permute-start.1
  20.4 7.9 %copy.77 = f32[1,5,12,16,128]{1,4,3,2,0:T(8,128)} copy(f32[1,5,12,16,128]{4,3,2,1,0:T(8,128)} %param.14) | data formatting | bytes 983040 | tf_op args[0]
  29.7 32.5 %gather_fusion.1 = f32[8192,5]{1,0:T(8,128)} fusion(f32[5,24576]{0,1:T(8,128)} %bitcast.63, s32[8192]{0:T(1024)S(1)} %fusion.153), kind=kCustom, calls=%fused_computation.1.clone | custom fusion | bytes 360448 | tf_op jit(solution)/shard_map/jit(_take)/gather | solution.py:110
  62.1 7.5 %broadcast_select_fusion.1 = f32[8192,5]{1,0:T(8,128)} fusion(f32[8192,5]{1,0:T(8,128)} %gather_fusion.1, pred[8192]{0:T(1024)(128)(4,1)S(1)} %compare_and_fusion), kind=kLoop, calls=%fused_computation.11 | loop fusion | flops 40960 | bytes 335872 | tf_op jit(solution)/shard_map/jit(_take)/select_n | solution.py:110
  69.6 2.9 copy.79
  73.4 40.1 %all-gather = f32[40,16,8]{1,2,0:T(8,128)S(1)} all-gather(f32[5,16,8]{1,2,0:T(8,128)S(1)} %copy.80), channel_id=2, replica_groups=mesh['dom'=8,'orb'=64] {'dom'}, dimensions={0}, use_global_device_ids=true | all-gather | bytes 23040 | tf_op jit(solution)/shard_map/all_gather | solution.py:113
  114.8 2.6 copy.83
  117.4 54.2 %scatter_custom_fusion = f32[5,24576]{0,1:T(8,128)} fusion(s32[8192]{0:T(1024)S(1)} %bitcast.80, f32[8192,5]{1,0:T(8,128)} %copy.83, f32[]{:T(128)} %constant.128.clone.1), kind=kCustom, calls=%fused_computation.8 | custom fusion | flops 40960 | bytes 492032 | tf_op jit(solution)/shard_map/scatter-add | solution.py:128
  171.7 8.3 %copy.84 = f32[5,12,16,128]{3,2,0,1:T(8,128)} copy(f32[5,12,16,128]{0,3,2,1:T(8,128)} %bitcast.60) | data formatting | bytes 983040 | tf_op jit(solution)/shard_map/reshape | solution.py:130
  182.5 7.0 %fusion.164 = (bf16[5,12,16,128]{3,2,0,1:T(8,128)(2,1)S(1)}, f32[5,12,16,128]{3,2,0,1:T(8,128)S(1)}) fusion(f32[5,12,16,128]{3,2,0,1:T(8,128)S(1)} %bitcast.68, f32[5,12,16,128]{3,2,0,1:T(8,128)} %copy.84, f32[12,16,128]{2,1,0:T(8,128)} %bitcast.79, f32[5,12,16,6]{3,2,0,1:T(8,128)} %get-tuple-element.22, f32[5,12,16,6]{3,2,0,1:T(8,128)} %get-tuple-element.21, ...), kind=kLoop, calls=%fused_computation.307 | loop fusion | flops 10690560 | bytes 8131584 | tf_op jit(solution)/shard_map/convert_element_type | solution.py:60
  189.7 2.1 collective-permute-start.3
  191.9 6.6 %copy.97 = f32[5,12,16,128]{0,3,2,1:T(8,128)} copy(f32[5,12,16,128]{3,2,0,1:T(8,128)S(1)} %broadcast_multiply_fusion) | data formatting | bytes 983040 | tf_op jit(solution)/shard_map/reshape | solution.py:108
  198.5 32.5 %gather_fusion.3 = f32[8192,5]{1,0:T(8,128)} fusion(f32[5,24576]{0,1:T(8,128)} %bitcast.64, s32[8192]{0:T(1024)S(1)} %fusion.153), kind=kCustom, calls=%fused_computation.3.clone | custom fusion | bytes 360448 | tf_op jit(solution)/shard_map/jit(_take)/gather | solution.py:110
  231.0 7.5 %broadcast_select_fusion = f32[8192,5]{1,0:T(8,128)} fusion(f32[8192,5]{1,0:T(8,128)} %gather_fusion.3, pred[8192]{0:T(1024)(128)(4,1)S(1)} %compare_and_fusion), kind=kLoop, calls=%fused_computation.10 | loop fusion | flops 40960 | bytes 335872 | tf_op jit(solution)/shard_map/jit(_take)/select_n | solution.py:110
  238.4 2.8 copy.88
  242.0 40.4 %all-gather.1 = f32[40,16,8]{1,2,0:T(8,128)S(1)} all-gather(f32[5,16,8]{1,2,0:T(8,128)S(1)} %copy.89), channel_id=3, replica_groups=mesh['dom'=8,'orb'=64] {'dom'}, dimensions={0}, use_global_device_ids=true | all-gather | bytes 23040 | tf_op jit(solution)/shard_map/all_gather | solution.py:113
  283.8 1.9 collective-permute-start.5
  285.8 2.6 copy.91
  288.5 54.2 %scatter_custom_fusion.1 = f32[5,24576]{0,1:T(8,128)} fusion(s32[8192]{0:T(1024)} %bitcast.81, f32[8192,5]{1,0:T(8,128)} %copy.91, f32[]{:T(128)} %constant.128.clone.1), kind=kCustom, calls=%fused_computation.6 | custom fusion | flops 40960 | bytes 492032 | tf_op jit(solution)/shard_map/scatter-add | solution.py:128
  342.7 7.6 %copy.93 = f32[5,12,16,128]{3,2,0,1:T(8,128)S(1)} copy(f32[5,12,16,128]{0,3,2,1:T(8,128)} %bitcast.59) | data formatting | bytes 983040 | tf_op jit(solution)/shard_map/reshape | solution.py:130
  350.3 2.4 collective-permute-start.4
  352.7 1.1 fusion.169
  353.8 6.0 %collective-permute-done.4 = bf16[5,12,12,128]{3,2,0,1:T(8,128)(2,1)S(1)} collective-permute-done((bf16[5,12,12,128]{3,2,0,1:T(8,128)(2,1)S(1)}, bf16[5,12,12,128]{3,2,0,1:T(8,128)(2,1)S(1)}, u32[]{:S(2)}, u32[]{:S(2)}) %collective-permute-start.4) | collective-permute-done | bytes 184352 | tf_op jit(solution)/shard_map/ppermute | solution.py:31
  361.6 1.1 copy.85
  362.7 1.9 gather_fusion.2
  364.6 7.5 %subtract_convert_fusion = bf16[5,12,16,128]{3,2,0,1:T(8,128)(2,1)S(1)} fusion(f32[5,12,16,128]{3,2,0,1:T(8,128)S(1)} %get-tuple-element.8, f32[5,12,16,128]{3,2,0,1:T(8,128)S(1)} %copy.93, f32[5,12,16,128]{3,2,0,1:T(8,128)S(1)} %broadcast_multiply_fusion, f32[5,12,16,6]{3,2,0,1:T(8,128)} %get-tuple-element.14, f32[5,12,16,6]{3,2,0,1:T(8,128)} %get-tuple-element.13, ...), kind=kLoop, calls=%fused_computation.265 | loop fusion | flops 10813440 | bytes 8623104 | tf_op jit(solution)/shard_map/convert_element_type | solution.py:175
  373.2 29.4 %all-to-all-start = ((bf16[5,64,384]{2,0,1:T(8,128)(2,1)}), bf16[5,64,384]{2,0,1:T(8,128)(2,1)S(1)}, u32[]{:S(2)}, u32[]{:S(2)}) async-start(bf16[5,64,384]{2,0,1:T(8,128)(2,1)} %copy.95), calls=%async_computation | async-start | bytes 786432 | tf_op jit(solution)/shard_map/all_to_all | solution.py:176
  402.6 170.0 %all-gather.2 = bf16[64,5,320]{2,1,0:T(8,128)(2,1)S(1)} all-gather(bf16[1,5,320]{2,1,0:T(8,128)(2,1)} %bitcast.82), channel_id=1, replica_groups=mesh['dom'=8,'orb'=64] {'orb'}, dimensions={0}, use_global_device_ids=true | all-gather | bytes 208000 | tf_op jit(solution)/shard_map/all_gather | solution.py:177
  573.4 23.8 %all_to_all.35 = bf16[64,5,384]{2,1,0:T(8,128)(2,1)S(1)} all-to-all(bf16[64,5,384]{2,1,0:T(8,128)(2,1)S(1)} %all_to_all.30), channel_id=1, replica_groups=mesh['dom'=8,'orb'=64] {'orb'}, dimensions={0} | all-to-all | bytes 491520 | tf_op jit(solution)/shard_map/all_to_all | solution.py:181
  (85 shorter events, 13.9 us)
Async XLA Ops:
  0.0 72.7 %copy-start = (f32[16,8,512]{2,1,0:T(8,128)S(1)}, f32[16,8,512]{2,1,0:T(8,128)}, u32[]{:S(2)}) copy-start(f32[16,8,512]{2,1,0:T(8,128)} %param.16) | copy-start | bytes 786436
  1.1 180.6 %collective-permute-start = (bf16[5,12,16,128]{3,2,0,1:T(8,128)(2,1)S(1)}, bf16[5,12,16,128]{3,2,0,1:T(8,128)(2,1)S(1)}, u32[]{:S(2)}, u32[]{:S(2)}) collective-permute-start(bf16[5,12,16,128]{3,2,0,1:T(8,128)(2,1)S(1)} %bitcast.69), channel_id=1, source_target_pairs={{0,64},{64,0},{128,192},{192,128},{256,320},{320,256},{384,448},{4... | collective-permute-start | bytes 737288 | tf_op jit(solution)/shard_map/ppermute | solution.py:31
  5.8 174.2 %collective-permute-start.2 = (bf16[5,12,16,12]{3,2,0,1:T(8,128)(2,1)S(1)}, bf16[5,12,16,12]{3,2,0,1:T(8,128)(2,1)S(1)}, u32[]{:S(2)}, u32[]{:S(2)}) collective-permute-start(bf16[5,12,16,12]{3,2,0,1:T(8,128)(2,1)S(1)} %pad_maximum_fusion.11), channel_id=1, source_target_pairs={{0,256},{256,0},{64,320},{320,64},{128,384},{384,128},{192,448},{4... | collective-permute-start | bytes 69128 | tf_op jit(solution)/shard_map/ppermute | solution.py:31
  15.5 165.6 %collective-permute-start.1 = (bf16[5,12,12,128]{3,2,0,1:T(8,128)(2,1)}, bf16[5,12,12,128]{3,2,0,1:T(8,128)(2,1)S(1)}, u32[]{:S(2)}, u32[]{:S(2)}) collective-permute-start(bf16[5,12,12,128]{3,2,0,1:T(8,128)(2,1)} %pad_maximum_fusion.10), channel_id=1, source_target_pairs={{0,128},{128,0},{64,192},{192,64},{256,384},{384,256},{320,448},{4... | collective-permute-start | bytes 552968 | tf_op jit(solution)/shard_map/ppermute | solution.py:31
  20.4 7.9 %copy-start.6 = (s32[16]{0:T(128)S(1)}, s32[16]{0:T(128)}, u32[]{:S(2)}) copy-start(s32[16]{0:T(128)} %param.18) | copy-start | bytes 196
  20.4 7.9 %copy-start.7 = (s32[16]{0:T(128)S(1)}, s32[16]{0:T(128)}, u32[]{:S(2)}) copy-start(s32[16]{0:T(128)} %param.20) | copy-start | bytes 196
  20.4 7.9 %copy-start.8 = (s32[16]{0:T(128)S(1)}, s32[16]{0:T(128)}, u32[]{:S(2)}) copy-start(s32[16]{0:T(128)} %param.19) | copy-start | bytes 196
  29.7 87.8 %copy-start.4 = (s32[8192,1]{0,1:T(1,128)}, s32[8192,1]{0,1:T(1,128)S(1)}, u32[]{:S(2)}) copy-start(s32[8192,1]{0,1:T(1,128)S(1)} %compare_select_fusion) | copy-start | bytes 98308
  69.6 43.9 %copy-start.9 = (f32[8]{0:T(128)S(1)}, f32[8]{0:T(128)}, u32[]{:S(2)}) copy-start(f32[8]{0:T(128)} %param.17) | copy-start | bytes 100
  69.6 44.5 %copy-start.2 = (f32[1,12,16,128]{3,2,1,0:T(8,128)S(1)}, f32[1,12,16,128]{3,2,1,0:T(8,128)}, u32[]{:S(2)}) copy-start(f32[1,12,16,128]{3,2,1,0:T(8,128)} %param.15) | copy-start | bytes 294916
  69.6 45.1 %copy-start.10 = (s32[24]{0:T(128)S(1)}, s32[24]{0:T(128)}, u32[]{:S(2)}) copy-start(s32[24]{0:T(128)} %constant.176) | copy-start | bytes 292
  69.6 45.1 %copy-start.1 = (f32[1,5,12,16,128]{4,3,2,1,0:T(8,128)S(1)}, f32[1,5,12,16,128]{4,3,2,1,0:T(8,128)}, u32[]{:S(2)}) copy-start(f32[1,5,12,16,128]{4,3,2,1,0:T(8,128)} %param.14) | copy-start | bytes 1474564
  114.8 67.1 %copy-start.5 = (s32[1024]{0:T(1024)}, s32[1024]{0:T(1024)S(1)}, u32[]{:S(2)}) copy-start(s32[1024]{0:T(1024)S(1)} %pad_clamp_fusion) | copy-start | bytes 12292
  189.7 170.8 %collective-permute-start.3 = (bf16[5,12,16,128]{3,2,0,1:T(8,128)(2,1)S(1)}, bf16[5,12,16,128]{3,2,0,1:T(8,128)(2,1)}, u32[]{:S(2)}, u32[]{:S(2)}) collective-permute-start(bf16[5,12,16,128]{3,2,0,1:T(8,128)(2,1)S(1)} %get-tuple-element.6), channel_id=1, source_target_pairs={{0,64},{64,0},{128,192},{192,128},{256,320},{320,256},{384,448},{4... | collective-permute-start | bytes 737288 | tf_op jit(solution)/shard_map/ppermute | solution.py:31
  283.8 68.9 %collective-permute-start.5 = (bf16[5,12,16,12]{3,2,0,1:T(8,128)(2,1)}, bf16[5,12,16,12]{3,2,0,1:T(8,128)(2,1)S(1)}, u32[]{:S(2)}, u32[]{:S(2)}) collective-permute-start(bf16[5,12,16,12]{3,2,0,1:T(8,128)(2,1)} %pad_maximum_fusion.13), channel_id=1, source_target_pairs={{0,256},{256,0},{64,320},{320,64},{128,384},{384,128},{192,448},{4... | collective-permute-start | bytes 69128 | tf_op jit(solution)/shard_map/ppermute | solution.py:31
  350.3 9.5 %collective-permute-start.4 = (bf16[5,12,12,128]{3,2,0,1:T(8,128)(2,1)S(1)}, bf16[5,12,12,128]{3,2,0,1:T(8,128)(2,1)S(1)}, u32[]{:S(2)}, u32[]{:S(2)}) collective-permute-start(bf16[5,12,12,128]{3,2,0,1:T(8,128)(2,1)S(1)} %pad_maximum_fusion.12), channel_id=1, source_target_pairs={{0,128},{128,0},{64,192},{192,64},{256,384},{384,256},{320,448},{4... | collective-permute-start | bytes 552968 | tf_op jit(solution)/shard_map/ppermute | solution.py:31
  353.7 10.9 %copy-start.3 = (f32[12,16,128]{2,1,0:T(8,128)S(1)}, f32[12,16,128]{2,1,0:T(8,128)}, u32[]{:S(2)}) copy-start(f32[12,16,128]{2,1,0:T(8,128)} %broadcast_multiply_fusion.1) | copy-start | bytes 294916
  373.2 199.6 %all-to-all-start = ((bf16[5,64,384]{2,0,1:T(8,128)(2,1)}), bf16[5,64,384]{2,0,1:T(8,128)(2,1)S(1)}, u32[]{:S(2)}, u32[]{:S(2)}) async-start(bf16[5,64,384]{2,0,1:T(8,128)(2,1)} %copy.95), calls=%async_computation | async-start | bytes 786432 | tf_op jit(solution)/shard_map/all_to_all | solution.py:176
